TPU v7x, 32 devices: a whole 2x2x4 slice. The times are simulated.
32 devices in a mesh: grp: 4 (over y, x), dev: 8 (over z, core).
Axes of the slice: x: 2, y: 2, z: 4, core: 2. Of those that a mesh axis runs over, the one named last changes fastest.
Arguments:
- tiles: bfloat16 [128, 9, 4, 4, 128], P(('grp', 'dev')), may hold values from -6 to 6
- cotangent: bfloat16 [128, 9, 8, 8, 128], P(('grp', 'dev')), may hold values from -6 to 6
- weight: bfloat16 [3456, 128], P('dev'), may hold values from -0.109375 to 0.109375
- bias: float32 [128], replicated, may hold values from -4 to 4
- counts: int32 [32], replicated, may hold values from 1 to 4, as said below
Outputs:
- grad_weight: float32 [3456, 128], P('dev')
- grad_bias: float32 [128], P('dev')
Inputs may be any that keep to these rules, and one draw needn't show every extreme that they name: `counts`: every group of 8 devices has at least one device with 4 live tiles; live tiles fill the first slots of a device.
All inputs are finite; a program needn't handle non-finite values.
Results may differ from a plain program's by a relative error of at most 0.0049.
Values may be sent and summed in bfloat16 or wider, within the bound.
A program may use at most 64 MiB of HBM per device.

v0:
```python
import math

import jax
import jax.numpy as jnp
from jax import lax
from jax.sharding import PartitionSpec as P


def padded_input(tile):
    up = jnp.repeat(jnp.repeat(tile, 2, axis=1), 2, axis=2)
    up = jnp.concatenate([up[:1], up[:1], up], axis=0)
    return jnp.pad(up, ((0, 0), (1, 1), (1, 1), (0, 0)))


def window_list(padded, frames, height, width):
    chans = padded.shape[-1]
    result = []
    for kd in range(3):
        for kh in range(3):
            for kw in range(3):
                piece = padded[kd : kd + frames, kh : kh + height, kw : kw + width, :]
                result.append(piece.reshape(frames * height * width, chans))
    return result


def tile_terms(tile, cot, taps, bias):
    frames, height, width = (tile.shape[0], 2 * tile.shape[1], 2 * tile.shape[2])
    windows = window_list(padded_input(tile), frames, height, width)
    z = jnp.zeros((frames * height * width, taps.shape[2]), jnp.float32) + bias
    for k in range(27):
        z = z + jnp.dot(windows[k], taps[k], preferred_element_type=jnp.float32)
    sig = jax.nn.sigmoid(z)
    dz = (cot.reshape(z.shape).astype(jnp.float32) * sig * (1.0 + z * (1.0 - sig))).astype(
        jnp.bfloat16
    )
    grads = [
        lax.dot_general(
            windows[k], dz, (((0,), (0,)), ((), ())), preferred_element_type=jnp.float32
        )
        for k in range(27)
    ]
    return (jnp.stack(grads, 0), jnp.sum(dz.astype(jnp.float32), axis=0))


def body(tiles, cotangent, weight, bias, counts):
    num_dev = lax.axis_size("dev")
    num_grp = lax.axis_size("grp")
    cap = tiles.shape[0]
    cin = tiles.shape[-1]
    cout = weight.shape[1]
    gathered = lax.all_gather(weight, "dev", axis=0, tiled=True)
    taps = gathered.reshape(cin, 27, cout).transpose(1, 0, 2)
    my_dev = lax.axis_index("dev")
    my_grp = lax.axis_index("grp")
    group_counts = lax.dynamic_slice_in_dim(counts, my_grp * num_dev, num_dev)
    my_count = group_counts[my_dev]

    def accumulate(index, carry):
        tile = lax.dynamic_index_in_dim(tiles, index, 0, keepdims=False)
        cot = lax.dynamic_index_in_dim(cotangent, index, 0, keepdims=False)
        gw, gb = tile_terms(tile, cot, taps, bias)
        return (carry[0] + gw, carry[1] + gb)

    init = (jnp.zeros((27, cin, cout), jnp.float32), jnp.zeros((cout,), jnp.float32))
    gw, gb = lax.fori_loop(0, my_count, accumulate, init)
    cells = tiles.shape[1] * 4 * tiles.shape[2] * tiles.shape[3]
    scale = 1.0 / math.sqrt(cap * num_dev * num_grp * cells)
    flat = gw.transpose(1, 0, 2).reshape(cin * 27, cout)
    rows = cin * 27 // num_dev
    share = cout // num_dev
    total_w, total_b = lax.psum((flat, gb), ("grp", "dev"))
    part_w = lax.dynamic_slice_in_dim(total_w, my_dev * rows, rows, 0)
    part_b = lax.dynamic_slice_in_dim(total_b, my_dev * share, share, 0)
    return (part_w * scale, part_b * scale)


def solution(mesh):
    return jax.shard_map(
        body,
        mesh=mesh,
        in_specs=(
            P(("grp", "dev"), None, None, None, None),
            P(("grp", "dev"), None, None, None, None),
            P("dev", None),
            P(),
            P(),
        ),
        out_specs=(P("dev", None), P("dev")),
        check_vma=False,
    )
```

profile of v0, /device:TPU:0, one launch (start us, length us, event | category | flops | bytes accessed | tf_op | source)
XLA Modules:
  0.0 237.2 jit_solution(10512830038723786257)
XLA Ops:
  7.2 17.7 %all_gather.3 = bf16[3456,128]{1,0:T(8,128)(2,1)S(1)} all-gather(bf16[432,128]{1,0:T(8,128)(2,1)} %param.9), channel_id=1, replica_groups=mesh['grp'=4,'dev'=8] {'dev'}, dimensions={0}, use_global_device_ids=true | all-gather | bytes 995328 | tf_op jit(solution)/shard_map/all_gather | solution.py:51
  25.0 0.3 reshape.213
  25.3 0.4 copy.8
  25.6 0.6 dynamic_slice.27
  26.4 17.0 %while.14 = (s32[]{:T(128)}, f32[27,128,128]{2,1,0:T(8,128)S(1)}, f32[128]{0:T(128)S(1)}, s32[]{:T(128)}, bf16[4,9,4,4,128]{4,3,2,1,0:T(4,128)(2,1)}, /*index=5*...) while((s32[]{:T(128)}, f32[27,128,128]{2,1,0:T(8,128)S(1)}, ...), condition=%wide.region_2.3_spmd, body=%wide.region_0.2_spmd.sunk | while | flops 1022787584 | bytes 41134752 | solution.py:65
  27.1 0.7 dynamic-slice_bitcast_fusion.5
  27.8 0.8 dynamic-slice_bitcast_fusion.4
  28.8 0.9 constant_dynamic-slice_fusion.2
  30.1 0.6 pad_slice_fusion.27
  35.3 0.3 convert_reduce_fusion.2
  36.1 0.3 fusion.407
  37.3 0.3 fusion.412
  37.6 0.3 fusion.413
  39.1 0.3 fusion.419
  39.3 0.3 fusion.420
  40.8 0.3 fusion.426
  41.1 0.3 fusion.427
  42.4 0.5 add.324
  43.5 2.4 %copy.9 = f32[128,27,128]{2,1,0:T(8,128)} copy(f32[128,27,128]{2,0,1:T(8,128)S(1)} %bitcast.654) | data formatting | bytes 3538944 | tf_op jit(solution)/shard_map/transpose | solution.py:68
  45.9 2.6 %reshape.214 = f32[3456,128]{1,0:T(8,128)} reshape(f32[128,27,128]{2,1,0:T(8,128)} %copy.9) | data formatting | bytes 3538944 | tf_op jit(solution)/shard_map/reshape | solution.py:68
  48.5 88.4 %psum.15 = f32[128]{0:T(128)S(1)} all-reduce(f32[128]{0:T(128)S(1)} %get-tuple-element.108), channel_id=1, replica_groups=mesh['grp'=4,'dev'=8] {'grp','dev'}, use_global_device_ids=true, to_apply=%region_4.5 | all-reduce | flops 128 | bytes 1024 | tf_op jit(solution)/shard_map/psum | solution.py:71
  136.8 0.6 dynamic-slice_multiply_fusion.1
  137.4 91.3 %all-reduce.3.cloned.1.call-done = f32[3456,128]{1,0:T(8,128)} async-done(((f32[3456,128]{1,0:T(8,128)}), f32[3456,128]{1,0:T(8,128)}) %all-reduce.3.cloned.1.call-update) | async-done | bytes 1769488 | tf_op jit(solution)/shard_map/psum | solution.py:71
  228.7 1.6 dynamic-slice_multiply_fusion
  (62 shorter events, 10.1 us)
Async XLA Ops:
  7.2 221.5 %all-reduce.3.cloned.1.call-start = ((), (), s32[]{:S(2)}) async-start(), calls=%async_computation | async-start | bytes 3538944 | tf_op jit(solution)/shard_map/psum | solution.py:71
  25.0 0.7 copy-start.1
  25.2 1.2 copy-start
Sparse Core Ops, SparseCore 0:
  48.6 180.0 all-reduce.2
where the time goes:
time: 238 us; the launch traced here: 237 us
  blocking collectives  106 us (45%)
  waiting for transfers between devices  91.3 us (38%)
  between operations  14.1 us (6%)
  matrix products  11.6 us (5%)
  local copies, waits for them, and re-layouts  9.7 us (4%)
  other arithmetic  2.72 us (1%)
    psum x1, waiting for transfers between devices, body(): total_w, total_b = lax.psum((flat, gb), ('grp', 'dev'))  91.3 us
    psum x1, blocking collectives, body(): total_w, total_b = lax.psum((flat, gb), ('grp', 'dev'))  88.4 us
    all_gather x1, blocking collectives, body(): gathered = lax.all_gather(weight, 'dev', axis=0, tiled=True)  17.7 us
    dot_general x27, matrix products, tile_terms(): lax.dot_general(windows[k], dz, (((0,), (0,)), ((), ())), preferred_eleme...  6.73 us
    dot_general x27, matrix products, tile_terms(): z = z + jnp.dot(windows[k], taps[k], preferred_element_type=jnp.float32)  4.87 us
  transfers between devices with their start and end apart: 1, of which 1 were waited for; matrix products, arithmetic and copies ran while one was open for 0% of the time, Pallas kernels for 0%

commit v1 on v0

v1 whole, which is shorter than its diff:
```python
import functools
import math

import jax
import jax.numpy as jnp
from jax import lax
from jax.experimental import pallas as pl
from jax.experimental.pallas import tpu as pltpu
from jax.sharding import PartitionSpec as P

MESH = pl.DeviceIdType.MESH
TAPS = {(0, 0): (0,), (0, 1): (1, 2), (1, 0): (0, 1), (1, 1): (2,)}
OFFSET = ((0, 1, 1), (0, 0, 1))


def terms_kernel(w_ref, x_ref, cot_ref, bias_ref, out_ref, wz_ref, g_ref):
    chans = 128
    slab = x_ref.shape[0] // 6
    rows = 4 * slab
    cols = ((0, 256), (0, 512), (256, 256))

    wz_ref[...] = jnp.zeros_like(wz_ref)
    for kd in range(3):
        tap = {}
        for kh in range(3):
            for kw in range(3):
                piece = w_ref[:, 9 * kd + 3 * kh + kw]
                tap[kh, kw] = piece.reshape(chans, chans).astype(jnp.float32)
        for ph in range(2):
            for a in range(2):
                line = [sum(tap[kh, kw] for kh in TAPS[ph, a]) for kw in range(3)]
                for pw in range(2):
                    for b in range(2):
                        both = sum(line[kw] for kw in TAPS[pw, b])
                        row = (b + pw) * 384 + kd * 128
                        col = (2 * ph + pw) * 128
                        wz_ref[a + ph, row : row + 128, col : col + 128] = both.astype(
                            jnp.bfloat16
                        )

    def window(dh):
        return x_ref[dh * slab : dh * slab + rows, :]

    mid = jnp.dot(window(1), wz_ref[1], preferred_element_type=jnp.float32)
    top = jnp.dot(window(0), wz_ref[0, :, 0:256], preferred_element_type=jnp.float32)
    low = jnp.dot(window(2), wz_ref[2, :, 256:512], preferred_element_type=jnp.float32)
    parts = []
    total_b = jnp.zeros((1, chans), jnp.float32)
    for p in range(4):
        side = (top if p < 2 else low)[:, (p % 2) * 128 : (p % 2) * 128 + 128]
        z = mid[:, p * 128 : p * 128 + 128] + side + bias_ref[...]
        sig = jax.nn.sigmoid(z)
        dz = cot_ref[p].astype(jnp.float32) * sig * (1.0 + z * (1.0 - sig))
        dz = dz.astype(jnp.bfloat16)
        total_b += jnp.sum(dz.astype(jnp.float32), axis=0, keepdims=True)
        parts.append(dz)
    dz = jnp.concatenate(parts, axis=1)
    for dh in range(3):
        start, width = cols[dh]
        g_ref[dh, :, start : start + width] = lax.dot_general(
            window(dh),
            dz[:, start : start + width],
            (((0,), (0,)), ((), ())),
            preferred_element_type=jnp.float32,
        )
    for kd in range(3):
        for kh in range(3):
            for kw in range(3):
                total = None
                for ph in range(2):
                    for pw in range(2):
                        row = (OFFSET[pw][kw] + pw) * 384 + kd * 128
                        col = (2 * ph + pw) * 128
                        term = g_ref[
                            OFFSET[ph][kh] + ph, row : row + 128, col : col + 128
                        ]
                        total = term if total is None else total + term
                out_ref[:, 9 * kd + 3 * kh + kw] = total.reshape(8, 16, chans)
    out_ref[:, 27] = jnp.broadcast_to(total_b.reshape(1, 1, chans), (8, 16, chans))


def terms(w, xs, cot, bias):
    flops = 2 * 2 * 576 * 1152 * 1024
    return pl.pallas_call(
        terms_kernel,
        out_shape=jax.ShapeDtypeStruct((8, 28, 16, 128), jnp.float32),
        in_specs=[pl.BlockSpec(memory_space=pltpu.VMEM)] * 4,
        out_specs=pl.BlockSpec(memory_space=pltpu.VMEM),
        scratch_shapes=[
            pltpu.VMEM((3, 1152, 512), jnp.bfloat16),
            pltpu.VMEM((3, 1152, 512), jnp.float32),
        ],
        compiler_params=pltpu.CompilerParams(vmem_limit_bytes=48 * 2**20),
        cost_estimate=pl.CostEstimate(
            flops=flops, bytes_accessed=6 * 2**20, transcendentals=576 * 512
        ),
    )(w, xs, cot, bias)


def reduce_kernel(
    scale, x_ref, o_ref, s1, r1, s2, r2, keep, s3, r3, s4, r4,
    ss1, rs1, ss2, rs2, ss3, rs3, ss4, rs4,
):
    grp = lax.axis_index("grp")
    dev = lax.axis_index("dev")
    depth = dev // 2
    core = dev % 2
    f32, bf16 = jnp.float32, jnp.bfloat16
    pair = {"dev": depth * 2 + (1 - core)}
    across = [{"grp": (grp + k) % 4} for k in range(1, 4)]
    along = [{"dev": ((depth + k) % 4) * 2 + core} for k in range(1, 4)]

    barrier = pltpu.get_barrier_semaphore()
    for peer in [pair] + across + along:
        pl.semaphore_signal(barrier, inc=1, device_id=peer, device_id_type=MESH)

    def send(src, dst, ssem, rsem, peer):
        copy = pltpu.make_async_remote_copy(
            src_ref=src, dst_ref=dst, send_sem=ssem, recv_sem=rsem,
            device_id=peer, device_id_type=MESH,
        )
        copy.start()
        return copy

    copies = []
    first = []
    for k in range(4):
        taps = pl.ds(((grp + k + 1) % 4) * 7, 7)
        s1[k] = x_ref[:, 1 - core, taps].astype(bf16)
        if k == 0:
            pl.semaphore_wait(barrier, 7)
        first.append(send(s1.at[k], r1.at[k], ss1.at[k], rs1.at[k], pair))
    second = []
    for k in range(4):
        taps = pl.ds(((grp + k + 1) % 4) * 7, 7)
        first[k].wait_recv()
        total = x_ref[:, core, taps] + r1[k].astype(f32)
        if k < 3:
            s2[k] = total.astype(bf16)
            second.append(send(s2.at[k], r2.at[k], ss2.at[k], rs2.at[k], across[k]))
        else:
            keep[...] = total
    for k in range(3):
        second[k].wait_recv()
        keep[...] += r2[k].astype(f32)
    third = []
    for k in range(3):
        s3[k] = keep[(depth + k + 1) % 4].astype(bf16)
        third.append(send(s3.at[k], r3.at[k], ss3.at[k], rs3.at[k], along[k]))
    total = keep[depth]
    for k in range(3):
        third[k].wait_recv()
        total += r3[k].astype(f32)
    total = total * scale
    s4[...] = total
    fourth = [
        send(s4, r4.at[k], ss4.at[k], rs4.at[k], across[k]) for k in range(3)
    ]
    o_ref[grp] = total
    for k in range(3):
        fourth[k].wait_recv()
        o_ref[(grp + 3 - k) % 4] = r4[k]
    for copy in first + second + third + fourth:
        copy.wait_send()


def reduce_terms(parts, scale):
    bf16, f32 = jnp.bfloat16, jnp.float32
    sem = pltpu.SemaphoreType.DMA
    return pl.pallas_call(
        functools.partial(reduce_kernel, scale),
        out_shape=jax.ShapeDtypeStruct((4, 7, 16, 128), f32),
        in_specs=[pl.BlockSpec(memory_space=pltpu.VMEM)],
        out_specs=pl.BlockSpec(memory_space=pltpu.VMEM),
        scratch_shapes=[
            pltpu.VMEM((4, 4, 7, 16, 128), bf16),
            pltpu.VMEM((4, 4, 7, 16, 128), bf16),
            pltpu.VMEM((3, 4, 7, 16, 128), bf16),
            pltpu.VMEM((3, 4, 7, 16, 128), bf16),
            pltpu.VMEM((4, 7, 16, 128), f32),
            pltpu.VMEM((3, 7, 16, 128), bf16),
            pltpu.VMEM((3, 7, 16, 128), bf16),
            pltpu.VMEM((7, 16, 128), f32),
            pltpu.VMEM((3, 7, 16, 128), f32),
            sem((4,)), sem((4,)), sem((3,)), sem((3,)),
            sem((3,)), sem((3,)), sem((3,)), sem((3,)),
        ],
        compiler_params=pltpu.CompilerParams(
            collective_id=1, has_side_effects=True, vmem_limit_bytes=48 * 2**20
        ),
    )(parts.reshape(4, 2, 28, 16, 128))


def input_windows(tiles):
    xt = tiles.transpose(2, 3, 0, 1, 4)
    first = xt[:, :, :, :1]
    back1 = jnp.concatenate([first, xt[:, :, :, :-1]], axis=3)
    back2 = jnp.concatenate([first, first, xt[:, :, :, :-2]], axis=3)
    timed = jnp.concatenate([back2, back1, xt], axis=-1)
    padded = jnp.pad(timed, ((1, 1), (1, 1), (0, 0), (0, 0), (0, 0)))
    wide = jnp.concatenate([padded[:, dw : dw + 4] for dw in range(3)], axis=-1)
    return wide.reshape(-1, wide.shape[-1])


def body(tiles, cotangent, weight, bias, counts):
    num_dev = lax.axis_size("dev")
    num_grp = lax.axis_size("grp")
    cap, frames, hl, wl, cin = tiles.shape
    cout = weight.shape[1]
    my_dev = lax.axis_index("dev")
    my_grp = lax.axis_index("grp")
    scale = 1.0 / math.sqrt(cap * num_dev * num_grp * frames * 4 * hl * wl)

    mine = weight.reshape(cin // num_dev, 27, cout).transpose(1, 0, 2)
    gathered = lax.all_gather(mine, "dev", axis=0, tiled=False)
    if num_dev != 8:
        gathered = gathered.transpose(1, 0, 2, 3).reshape(27, 8, 16, cout)
        gathered = gathered.transpose(1, 0, 2, 3)

    xs = input_windows(tiles)
    my_count = counts[my_grp * num_dev + my_dev]
    live = (jnp.arange(cap, dtype=jnp.int32) < my_count).reshape(cap, 1, 1, 1, 1)
    cot = jnp.where(live, cotangent, jnp.zeros((), cotangent.dtype))
    cot = cot.reshape(cap, frames, hl, 2, wl, 2, cout).transpose(3, 5, 2, 4, 0, 1, 6)
    cot = cot.reshape(4, hl * wl * cap * frames, cout)

    parts = terms(gathered, xs, cot, bias.reshape(1, cout))
    share = cout // num_dev
    if (num_grp, num_dev) == (4, 8):
        done = reduce_terms(parts, scale).reshape(28, 16, cout)
        part_w = done[:27].transpose(1, 0, 2).reshape(432, cout)
        part_b = lax.dynamic_slice_in_dim(done[27, 0], my_dev * share, share, 0)
        return part_w, part_b
    flat = parts[:, :27].transpose(0, 2, 1, 3).reshape(cin * 27, cout)
    part_w = lax.psum_scatter(flat, "dev", scatter_dimension=0, tiled=True)
    part_w = lax.psum(part_w, "grp")
    total_b = lax.psum(parts[0, 27, 0], ("grp", "dev"))
    part_b = lax.dynamic_slice_in_dim(total_b, my_dev * share, share, 0)
    return part_w * scale, part_b * scale


def solution(mesh):
    return jax.shard_map(
        body,
        mesh=mesh,
        in_specs=(
            P(("grp", "dev"), None, None, None, None),
            P(("grp", "dev"), None, None, None, None),
            P("dev", None),
            P(),
            P(),
        ),
        out_specs=(P("dev", None), P("dev")),
        check_vma=False,
    )
```

time: 238 us -> 58 us (0.24)
  waiting for transfers between devices: 91.3 us -> 0 us
  blocking collectives: 106 us -> 17.5 us
  Pallas kernels: 0 us -> 24.8 us
  between operations: 14.1 us -> 0.8 us
  matrix products: 11.6 us -> 0 us
    psum x1 -> x0, waiting for transfers between devices: 91.3 us -> none  [body(): total_w, total_b = lax.psum((flat, gb), ('grp', 'dev'))]
    psum x1 -> x0, blocking collectives: 88.4 us -> none  [body(): total_w, total_b = lax.psum((flat, gb), ('grp', 'dev'))]
    pallas_call x0 -> x2, Pallas kernels: none -> 24.8 us  [the longest x1 20.6 us: reduce_terms(): pl.pallas_call(functools.partial(reduce_kernel, scale), out_shape=jax.Sha...]
    dot_general x54 -> x0, matrix products: 11.6 us -> none  [the longest x27 6.73 us: tile_terms(): lax.dot_general(windows[k], dz, (((0,), (0,)), ((), ())), preferred_eleme...]
    concatenate x0 -> x1, local copies, waits for them, and re-layouts: none -> 2.38 us  [input_windows(): wide = jnp.concatenate([padded[:, dw:dw + 4] for dw in range(3)], axis=-1)]
  transfers between devices with their start and end apart: 1 -> 0, of which waited for: 1 -> 0; matrix products, arithmetic and copies ran while one was open for 0% -> 0% of each run, Pallas kernels for 0% -> 0%
where the time goes in v1:
time: 58 us; the launch traced here: 57.7 us
  Pallas kernels  24.8 us (43%)
  blocking collectives  17.5 us (30%)
  local copies, waits for them, and re-layouts  11.5 us (20%)
  other arithmetic  3.1 us (5%)
  between operations  0.8 us (1%)
    pallas_call x1, Pallas kernels, reduce_terms(): pl.pallas_call(functools.partial(reduce_kernel, scale), out_shape=jax.Sha...  20.6 us
    all_gather x1, blocking collectives, body(): gathered = lax.all_gather(mine, 'dev', axis=0, tiled=False)  17.5 us
    pallas_call x1, Pallas kernels, terms(): pl.pallas_call(terms_kernel, out_shape=jax.ShapeDtypeStruct((8, 28, 16, 1...  4.15 us
    reshape x1, local copies, waits for them, and re-layouts, input_windows(): return wide.reshape(-1, wide.shape[-1])  3.18 us
    concatenate x1, local copies, waits for them, and re-layouts, input_windows(): wide = jnp.concatenate([padded[:, dw:dw + 4] for dw in range(3)], axis=-1)  2.38 us
    concatenate x1, other arithmetic, input_windows(): timed = jnp.concatenate([back2, back1, xt], axis=-1)  1.42 us

profile of v1, /device:TPU:0, one launch (start us, length us, event | category | flops | bytes accessed | tf_op | source)
XLA Modules:
  0.0 57.7 jit_solution(10122855216611841100)
XLA Ops:
  0.6 1.0 %slice.34 = bf16[4,4,4,8,128]{4,1,0,3,2:T(4,128)(2,1)S(1)} slice(bf16[4,4,4,9,128]{4,1,0,3,2:T(4,128)(2,1)} %bitcast.22), slice={[0:4], [0:4], [0:4], [0:8], [0:128]} | slice | bytes 262144 | tf_op jit(solution)/shard_map/slice | solution.py:197
  1.6 0.9 %slice.33 = bf16[4,4,4,7,128]{4,1,0,3,2:T(4,128)(2,1)S(1)} slice(bf16[4,4,4,9,128]{4,1,0,3,2:T(4,128)(2,1)} %bitcast.23), slice={[0:4], [0:4], [0:4], [0:7], [0:128]} | slice | bytes 229376 | tf_op jit(solution)/shard_map/slice | solution.py:198
  2.5 0.7 %slice.32 = bf16[4,4,4,1,128]{4,1,0,3,2:T(4,128)(2,1)S(1)} slice(bf16[4,4,4,9,128]{4,1,0,3,2:T(4,128)(2,1)} %bitcast.24), slice={[0:4], [0:4], [0:4], [0:1], [0:128]} | slice | bytes 32768 | tf_op jit(solution)/shard_map/slice | solution.py:196
  3.3 1.4 %select_maximum_fusion = bf16[6,6,4,9,384]{4,1,0,3,2:T(8,128)(2,1)S(1)} fusion(bf16[4,4,4,9,128]{4,1,0,3,2:T(4,128)(2,1)} %bitcast.25, bf16[4,4,4,8,128]{4,1,0,3,2:T(4,128)(2,1)S(1)} %slice.34, bf16[4,4,4,1,128]{4,1,0,3,2:T(4,128)(2,1)S(1)} %slice.32, bf16[4,4,4,7,128]{4,1,0,3,2:T(4,128)(2,1)S(1)} %slice.33), kind=kLoop, calls=%fused_computation.8 | loop fusion | flops 15427584 | bytes 1404928 | tf_op jit(solution)/shard_map/concatenate | solution.py:199
  4.7 0.7 %fusion.7 = (bf16[6,4,4,9,384]{4,1,0,3,2:T(4,128)(2,1)S(1)}, bf16[6,4,4,9,384]{4,1,0,3,2:T(4,128)(2,1)S(1)}, bf16[6,4,4,9,384]{4,1,0,3,2:T(4,128)(2,1)S(1)}) fusion(bf16[6,6,4,9,384]{4,1,0,3,2:T(8,128)(2,1)S(1)} %select_maximum_fusion), kind=kLoop, calls=%fused_computation.20 | loop fusion | bytes 3981312 | tf_op jit(solution)/shard_map/slice | solution.py:201
  5.4 0.9 %pad_maximum_fusion = bf16[6,4,4,9,1152]{4,1,0,3,2:T(4,128)(2,1)S(1)} fusion(bf16[6,4,4,9,384]{4,1,0,3,2:T(4,128)(2,1)S(1)} %get-tuple-element.4, bf16[6,4,4,9,384]{4,1,0,3,2:T(4,128)(2,1)S(1)} %get-tuple-element.3, bf16[6,4,4,9,384]{4,1,0,3,2:T(4,128)(2,1)S(1)} %get-tuple-element.2), kind=kLoop, calls=%fused_computation.7 | loop fusion | flops 5971968 | bytes 3981312 | tf_op jit(solution)/shard_map/concatenate | solution.py:201
  6.3 2.4 %copy.17 = bf16[6,4,4,9,1152]{4,3,2,1,0:T(8,128)(2,1)} copy(bf16[6,4,4,9,1152]{4,1,0,3,2:T(4,128)(2,1)S(1)} %pad_maximum_fusion) | data formatting | bytes 3981312 | tf_op jit(solution)/shard_map/concatenate | solution.py:201
  8.7 3.2 %reshape.35.x_ref = bf16[864,1152]{1,0:T(8,128)(2,1)S(1)} reshape(bf16[6,4,4,9,1152]{4,3,2,1,0:T(8,128)(2,1)} %copy.17) | data formatting | bytes 3981312 | tf_op jit(solution)/shard_map/reshape | solution.py:202
  11.9 0.0 copy-start.2
  11.9 0.0 copy-done.3
  11.9 0.6 %dynamic_slice.8 = s32[1]{0:T(128)} dynamic-slice(s32[32]{0:T(128)S(1)} %copy-done.3, s32[]{:T(128)S(6)} %select_n.10), dynamic_slice_sizes={1} | dynamic-slice | bytes 12 | tf_op jit(solution)/shard_map/dynamic_slice | solution.py:221
  12.5 0.6 %iota_compare_fusion.4 = pred[4]{0:T(512)(128)(4,1)S(1)} fusion(s32[]{:T(128)} %bitcast.3), kind=kLoop, calls=%fused_computation.19 | loop fusion | flops 4 | bytes 8 | tf_op jit(solution)/shard_map/lt | solution.py:222
  13.2 0.0 copy-done.1
  13.2 0.1 broadcast_select_fusion
  13.3 0.0 copy-start
  13.3 0.4 copy.18
  13.7 0.1 copy.19.cot_ref
  13.8 0.0 copy-done.2
  13.9 17.5 %all-gather = bf16[216,16,128]{2,1,0:T(8,128)(2,1)S(1)} all-gather(bf16[27,16,128]{2,1,0:T(8,128)(2,1)S(1)} %copy.16), channel_id=2, replica_groups=mesh['grp'=4,'dev'=8] {'dev'}, dimensions={0}, use_global_device_ids=true | all-gather | bytes 995328 | tf_op jit(solution)/shard_map/all_gather | solution.py:215
  31.5 4.2 %shard_map.68 = f32[8,28,16,128]{3,2,1,0:T(8,128)S(1)} custom-call(bf16[8,27,16,128]{3,2,1,0:T(8,128)(2,1)S(1)} %bitcast.18, bf16[864,1152]{1,0:T(8,128)(2,1)S(1)} %reshape.35.x_ref, bf16[4,576,128]{2,1,0:T(8,128)(2,1)S(1)} %copy.19.cot_ref, f32[1,128]{1,0:T(1,128)S(1)} %bitcast.19), custom_call_target="tpu_custom_call" | custom-call | flops 2717908992 | bytes 6291456 | tf_op jit(solution)/shard_map/pallas_call | solution.py:84
  35.6 20.6 %shard_map.69 = f32[4,7,16,128]{3,2,1,0:T(8,128)S(1)} custom-call(f32[4,2,28,16,128]{4,3,2,1,0:T(8,128)S(1)} %bitcast.15), custom_call_target="tpu_custom_call" | custom-call | tf_op jit(solution)/shard_map/pallas_call | solution.py:170
  56.3 0.6 %dynamic-slice_bitcast_fusion = f32[16]{0:T(128)} fusion(f32[1,1,128]{2,1,0:T(1,128)S(1)} %slice.39, s32[]{:T(128)S(6)} %select_n.12), kind=kLoop, calls=%fused_computation.18 | loop fusion | bytes 132 | tf_op jit(solution)/shard_map/dynamic_slice | solution.py:232
  56.9 0.1 copy.20
  57.0 0.7 %reshape.41 = f32[432,128]{1,0:T(8,128)} reshape(f32[16,27,128]{2,1,0:T(8,128)S(1)} %copy.20) | data formatting | bytes 442368 | tf_op jit(solution)/shard_map/reshape | solution.py:231
  (7 shorter events, 0.1 us)
Async XLA Ops:
  8.7 3.2 %copy-start.3 = (s32[32]{0:T(128)S(1)}, s32[32]{0:T(128)}, u32[]{:S(2)}) copy-start(s32[32]{0:T(128)} %param.9) | copy-start | bytes 388
  8.7 4.5 %copy-start.1 = (bf16[4,9,8,8,128]{4,3,2,1,0:T(8,128)(2,1)S(1)}, bf16[4,9,8,8,128]{4,3,2,1,0:T(8,128)(2,1)}, u32[]{:S(2)}) copy-start(bf16[4,9,8,8,128]{4,3,2,1,0:T(8,128)(2,1)} %param.6) | copy-start | bytes 1769476
  11.9 1.9 %copy-start.2 = (bf16[432,128]{1,0:T(8,128)(2,1)S(1)}, bf16[432,128]{1,0:T(8,128)(2,1)}, u32[]{:S(2)}) copy-start(bf16[432,128]{1,0:T(8,128)(2,1)} %param.7) | copy-start | bytes 331780
  13.3 18.2 %copy-start = (f32[128]{0:T(128)S(1)}, f32[128]{0:T(128)}, u32[]{:S(2)}) copy-start(f32[128]{0:T(128)} %param.8) | copy-start | bytes 1540

commit v2 on v1

v2 whole, which is shorter than its diff:
```python
import functools
import math

import jax
import jax.numpy as jnp
from jax import lax
from jax.experimental import pallas as pl
from jax.experimental.pallas import tpu as pltpu
from jax.sharding import PartitionSpec as P

MESH = pl.DeviceIdType.MESH
TAPS = {(0, 0): (0,), (0, 1): (1, 2), (1, 0): (0, 1), (1, 1): (2,)}
OFFSET = ((0, 1, 1), (0, 0, 1))


def build_windows(x_ref, f_ref, xs_ref):
    rows = x_ref.shape[0]
    slab = rows // 4
    pad = 40
    row = lax.broadcasted_iota(jnp.int32, (rows, 128), 0).astype(jnp.float32)
    frame = row - 9.0 * jnp.floor((row + 0.5) * (1.0 / 9.0))
    place = lax.broadcasted_iota(jnp.int32, (slab, 128), 0)
    xs_ref[0:slab] = jnp.zeros((slab, 1152), jnp.bfloat16)
    xs_ref[5 * slab : 6 * slab] = jnp.zeros((slab, 1152), jnp.bfloat16)
    f_ref[...] = jnp.zeros_like(f_ref)
    now = x_ref[...].astype(jnp.float32)
    f_ref[2, pad : pad + rows] = now
    back1 = jnp.where(frame < 0.5, now, f_ref[2, pad - 1 : pad - 1 + rows])
    f_ref[1, pad : pad + rows] = back1
    f_ref[0, pad : pad + rows] = jnp.where(
        frame < 1.5, back1, f_ref[2, pad - 2 : pad - 2 + rows]
    )
    for h in range(4):
        for dw in range(3):
            for kd in range(3):
                start = pad + h * slab + (dw - 1) * 36
                piece = f_ref[kd, start : start + slab]
                if dw == 0:
                    piece = jnp.where(place < 36, 0.0, piece)
                if dw == 2:
                    piece = jnp.where(place >= slab - 36, 0.0, piece)
                col = dw * 384 + kd * 128
                xs_ref[(h + 1) * slab : (h + 2) * slab, col : col + 128] = piece.astype(
                    jnp.bfloat16
                )


def combine_weights(w_ref, wz_ref):
    chans = 128
    for kd in range(3):
        tap = {}
        for kh in range(3):
            for kw in range(3):
                piece = w_ref[:, 9 * kd + 3 * kh + kw]
                tap[kh, kw] = piece.reshape(chans, chans).astype(jnp.float32)
        for ph in range(2):
            for a in range(2):
                line = [sum(tap[kh, kw] for kh in TAPS[ph, a]) for kw in range(3)]
                for pw in range(2):
                    for b in range(2):
                        both = sum(line[kw] for kw in TAPS[pw, b])
                        row = (b + pw) * 384 + kd * 128
                        col = (2 * ph + pw) * 128
                        wz_ref[a + ph, row : row + 128, col : col + 128] = both.astype(
                            jnp.bfloat16
                        )


def products(xs_ref, cot_ref, bias_ref, wz_ref, g_ref):
    slab = xs_ref.shape[0] // 6
    rows = 4 * slab
    cols = ((0, 256), (0, 512), (256, 256))

    def window(dh):
        return xs_ref[dh * slab : dh * slab + rows, :]

    mid = jnp.dot(window(1), wz_ref[1], preferred_element_type=jnp.float32)
    top = jnp.dot(window(0), wz_ref[0, :, 0:256], preferred_element_type=jnp.float32)
    low = jnp.dot(window(2), wz_ref[2, :, 256:512], preferred_element_type=jnp.float32)
    parts = []
    total_b = jnp.zeros((1, 128), jnp.float32)
    for p in range(4):
        side = (top if p < 2 else low)[:, (p % 2) * 128 : (p % 2) * 128 + 128]
        z = mid[:, p * 128 : p * 128 + 128] + side + bias_ref[...]
        sig = jax.nn.sigmoid(z)
        dz = cot_ref[p].astype(jnp.float32) * sig * (1.0 + z * (1.0 - sig))
        dz = dz.astype(jnp.bfloat16)
        total_b += jnp.sum(dz.astype(jnp.float32), axis=0, keepdims=True)
        parts.append(dz)
    dz = jnp.concatenate(parts, axis=1)
    for dh in range(3):
        start, width = cols[dh]
        g_ref[dh, :, start : start + width] = lax.dot_general(
            window(dh),
            dz[:, start : start + width],
            (((0,), (0,)), ((), ())),
            preferred_element_type=jnp.float32,
        )
    return total_b


def tap_gradient(g_ref, k):
    kd, kh, kw = k // 9, k // 3 % 3, k % 3
    total = None
    for ph in range(2):
        for pw in range(2):
            row = (OFFSET[pw][kw] + pw) * 384 + kd * 128
            col = (2 * ph + pw) * 128
            term = g_ref[OFFSET[ph][kh] + ph, row : row + 128, col : col + 128]
            total = term if total is None else total + term
    return total


WORK = [
    pltpu.VMEM((3, 656, 128), jnp.float32),
    pltpu.VMEM((864, 1152), jnp.bfloat16),
    pltpu.VMEM((3, 1152, 512), jnp.bfloat16),
    pltpu.VMEM((3, 1152, 512), jnp.float32),
]


def terms_kernel(w_ref, x_ref, cot_ref, bias_ref, out_ref, f_ref, xs_ref, wz_ref, g_ref):
    build_windows(x_ref, f_ref, xs_ref)
    wz_ref[...] = jnp.zeros_like(wz_ref)
    combine_weights(w_ref, wz_ref)
    total_b = products(xs_ref, cot_ref, bias_ref, wz_ref, g_ref)
    for k in range(27):
        out_ref[:, k] = tap_gradient(g_ref, k).reshape(8, 16, 128)
    out_ref[:, 27] = jnp.broadcast_to(total_b.reshape(1, 1, 128), (8, 16, 128))


def terms(w, x, cot, bias):
    return pl.pallas_call(
        terms_kernel,
        out_shape=jax.ShapeDtypeStruct((8, 28, 16, 128), jnp.float32),
        in_specs=[pl.BlockSpec(memory_space=pltpu.VMEM)] * 4,
        out_specs=pl.BlockSpec(memory_space=pltpu.VMEM),
        scratch_shapes=WORK,
        compiler_params=pltpu.CompilerParams(vmem_limit_bytes=48 * 2**20),
    )(w, x, cot, bias)


def whole_kernel(
    scale, w_ref, x_ref, cot_ref, bias_ref, o_ref, b_ref,
    f_ref, xs_ref, wz_ref, g_ref, w_all, parts,
    s1, r1, s2, r2, keep, s3, r3, s4, r4, sb, rb,
    sw1, rw1, sw2, rw2, ss1, rs1, ss2, rs2, ss3, rs3, ss4, rs4, ssb, rsb,
):
    grp = lax.axis_index("grp")
    dev = lax.axis_index("dev")
    depth = dev // 2
    core = dev % 2
    f32, bf16 = jnp.float32, jnp.bfloat16
    pair = {"dev": depth * 2 + (1 - core)}
    across = [{"grp": (grp + k) % 4} for k in range(1, 4)]
    along = [{"dev": ((depth + k) % 4) * 2 + core} for k in range(1, 4)]

    barrier = pltpu.get_barrier_semaphore()
    for peer in [pair] + across + along:
        pl.semaphore_signal(barrier, inc=1, device_id=peer, device_id_type=MESH)
    pl.semaphore_wait(barrier, 7)

    def send(src, dst, ssem, rsem, peer):
        copy = pltpu.make_async_remote_copy(
            src_ref=src, dst_ref=dst, send_sem=ssem, recv_sem=rsem,
            device_id=peer, device_id_type=MESH,
        )
        copy.start()
        return copy

    out = [
        send(w_ref, w_all.at[dev], sw1.at[k], rw1.at[k], along[k]) for k in range(3)
    ]
    swap = [send(w_ref, w_all.at[dev], sw2.at[3], rw2.at[3], pair)]
    w_all[dev] = w_ref[...]
    wz_ref[...] = jnp.zeros_like(wz_ref)
    build_windows(x_ref, f_ref, xs_ref)
    for k in (0, 2, 1):
        out[k].wait_recv()
        block = w_all.at[((depth + 3 - k) % 4) * 2 + core]
        swap.append(send(block, block, sw2.at[k], rw2.at[k], pair))
    for copy in swap:
        copy.wait_recv()
    combine_weights(w_all, wz_ref)
    total_b = products(xs_ref, cot_ref, bias_ref, wz_ref, g_ref)

    sb[0] = jnp.broadcast_to(total_b, (8, 128))
    bias_copies = [send(sb.at[0], rb.at[0], ssb.at[0], rsb.at[0], pair)]
    first = []
    for q in range(4):
        for k in range(7 * q, 7 * q + 7):
            if k < 27:
                parts[:, :, k] = tap_gradient(g_ref, k).reshape(4, 2, 16, 128)
            else:
                parts[:, :, k] = jnp.zeros((4, 2, 16, 128), f32)
        s1[q] = parts[:, 1 - core, 7 * q : 7 * q + 7].astype(bf16)
        first.append(send(s1.at[q], r1.at[q], ss1.at[q], rs1.at[q], pair))

    bias_copies[0].wait_recv()
    sb[1] = sb[0] + rb[0]
    for k in range(3):
        bias_copies.append(
            send(sb.at[1], rb.at[1 + k], ssb.at[1 + k], rsb.at[1 + k], across[k])
        )
    second = []
    for q in range(4):
        first[q].wait_recv()
    for k in range(4):
        q = (grp + k + 1) % 4
        total = parts[:, core, pl.ds(q * 7, 7)] + r1[q].astype(f32)
        if k < 3:
            s2[k] = total.astype(bf16)
            second.append(send(s2.at[k], r2.at[k], ss2.at[k], rs2.at[k], across[k]))
        else:
            keep[...] = total
    for k in range(3):
        bias_copies[1 + k].wait_recv()
    sb[2] = (sb[1] + rb[1]) + (rb[2] + rb[3])
    for k in range(3):
        bias_copies.append(
            send(sb.at[2], rb.at[4 + k], ssb.at[4 + k], rsb.at[4 + k], along[k])
        )
    for k in range(3):
        second[k].wait_recv()
        keep[...] += r2[k].astype(f32)
    third = []
    for k in range(3):
        s3[k] = keep[(depth + k + 1) % 4].astype(bf16)
        third.append(send(s3.at[k], r3.at[k], ss3.at[k], rs3.at[k], along[k]))
    for k in range(3):
        bias_copies[4 + k].wait_recv()
    b_ref[...] = ((sb[2] + rb[4]) + (rb[5] + rb[6])) * scale
    total = keep[depth]
    for k in range(3):
        third[k].wait_recv()
        total += r3[k].astype(f32)
    total = total * scale
    s4[...] = total
    fourth = [
        send(s4, r4.at[k], ss4.at[k], rs4.at[k], across[k]) for k in range(3)
    ]
    o_ref[grp] = total
    for k in range(3):
        fourth[k].wait_recv()
        o_ref[(grp + 3 - k) % 4] = r4[k]
    for copy in out + swap + bias_copies + first + second + third + fourth:
        copy.wait_send()


def whole(w, x, cot, bias, scale):
    bf16, f32 = jnp.bfloat16, jnp.float32
    sem = pltpu.SemaphoreType.DMA
    return pl.pallas_call(
        functools.partial(whole_kernel, scale),
        out_shape=(
            jax.ShapeDtypeStruct((4, 7, 16, 128), f32),
            jax.ShapeDtypeStruct((8, 128), f32),
        ),
        in_specs=[pl.BlockSpec(memory_space=pltpu.VMEM)] * 4,
        out_specs=[pl.BlockSpec(memory_space=pltpu.VMEM)] * 2,
        scratch_shapes=WORK
        + [
            pltpu.VMEM((8, 27, 16, 128), bf16),
            pltpu.VMEM((4, 2, 28, 16, 128), f32),
            pltpu.VMEM((4, 4, 7, 16, 128), bf16),
            pltpu.VMEM((4, 4, 7, 16, 128), bf16),
            pltpu.VMEM((3, 4, 7, 16, 128), bf16),
            pltpu.VMEM((3, 4, 7, 16, 128), bf16),
            pltpu.VMEM((4, 7, 16, 128), f32),
            pltpu.VMEM((3, 7, 16, 128), bf16),
            pltpu.VMEM((3, 7, 16, 128), bf16),
            pltpu.VMEM((7, 16, 128), f32),
            pltpu.VMEM((3, 7, 16, 128), f32),
            pltpu.VMEM((3, 8, 128), f32),
            pltpu.VMEM((7, 8, 128), f32),
            sem((3,)), sem((3,)), sem((4,)), sem((4,)),
            sem((4,)), sem((4,)), sem((3,)), sem((3,)),
            sem((3,)), sem((3,)), sem((3,)), sem((3,)),
            sem((7,)), sem((7,)),
        ],
        compiler_params=pltpu.CompilerParams(
            collective_id=1, has_side_effects=True, vmem_limit_bytes=48 * 2**20
        ),
    )(w, x, cot, bias)


def body(tiles, cotangent, weight, bias, counts):
    num_dev = lax.axis_size("dev")
    num_grp = lax.axis_size("grp")
    cap, frames, hl, wl, cin = tiles.shape
    cout = weight.shape[1]
    my_dev = lax.axis_index("dev")
    my_grp = lax.axis_index("grp")
    scale = 1.0 / math.sqrt(cap * num_dev * num_grp * frames * 4 * hl * wl)

    mine = weight.reshape(cin // num_dev, 27, cout).transpose(1, 0, 2)
    x = tiles.transpose(2, 3, 0, 1, 4).reshape(hl * wl * cap * frames, cin)
    my_count = counts[my_grp * num_dev + my_dev]
    live = (jnp.arange(cap, dtype=jnp.int32) < my_count).reshape(cap, 1, 1, 1, 1)
    cot = jnp.where(live, cotangent, jnp.zeros((), cotangent.dtype))
    cot = cot.reshape(cap, frames, hl, 2, wl, 2, cout).transpose(3, 5, 2, 4, 0, 1, 6)
    cot = cot.reshape(4, hl * wl * cap * frames, cout)

    share = cout // num_dev
    bias = bias.reshape(1, cout)
    if (num_grp, num_dev) == (4, 8):
        done, total_b = whole(mine, x, cot, bias, scale)
        done = done.reshape(28, 16, cout)
        part_w = done[:27].transpose(1, 0, 2).reshape(432, cout)
        part_b = lax.dynamic_slice_in_dim(total_b[0], my_dev * share, share, 0)
        return part_w, part_b
    gathered = lax.all_gather(mine, "dev", axis=0, tiled=False)
    if num_dev != 8:
        gathered = gathered.transpose(1, 0, 2, 3).reshape(27, 8, 16, cout)
        gathered = gathered.transpose(1, 0, 2, 3)
    parts = terms(gathered, x, cot, bias)
    flat = parts[:, :27].transpose(0, 2, 1, 3).reshape(cin * 27, cout)
    part_w = lax.psum_scatter(flat, "dev", scatter_dimension=0, tiled=True)
    part_w = lax.psum(part_w, "grp")
    total_b = lax.psum(parts[0, 27, 0], ("grp", "dev"))
    part_b = lax.dynamic_slice_in_dim(total_b, my_dev * share, share, 0)
    return part_w * scale, part_b * scale


def solution(mesh):
    return jax.shard_map(
        body,
        mesh=mesh,
        in_specs=(
            P(("grp", "dev"), None, None, None, None),
            P(("grp", "dev"), None, None, None, None),
            P("dev", None),
            P(),
            P(),
        ),
        out_specs=(P("dev", None), P("dev")),
        check_vma=False,
    )
```

time: 58 us -> 46.2 us (0.80)
  blocking collectives: 17.5 us -> 0 us
  Pallas kernels: 24.8 us -> 37.7 us
  local copies, waits for them, and re-layouts: 11.5 us -> 5.61 us
  other arithmetic: 3.1 us -> 1.83 us
    all_gather x1 -> x0, blocking collectives: 17.5 us -> none  [body(): gathered = lax.all_gather(mine, 'dev', axis=0, tiled=False)]
    pallas_call x2 -> x1, Pallas kernels: 24.8 us -> 37.7 us  [whole(): pl.pallas_call(functools.partial(whole_kernel, scale), out_shape=(jax.Sha...]
    slice x5 -> x2, local copies, waits for them, and re-layouts: 3.34 us -> 0.02 us  [the longest x1 0.02 us: body(): part_w = done[:27].transpose(1, 0, 2).reshape(432, cout)]
    reshape x1, local copies, waits for them, and re-layouts: 3.18 us -> 0.07 us  [body(): x = tiles.transpose(2, 3, 0, 1, 4).reshape(hl * wl * cap * frames, cin)]
    unnamed x8 -> x9, local copies, waits for them, and re-layouts: 0.02 us -> 3.01 us
    concatenate x1 -> x0, local copies, waits for them, and re-layouts: 2.38 us -> none  [input_windows(): wide = jnp.concatenate([padded[:, dw:dw + 4] for dw in range(3)], axis=-1)]
    concatenate x2 -> x0, other arithmetic: 2.34 us -> none  [the longest x1 1.42 us: input_windows(): timed = jnp.concatenate([back2, back1, xt], axis=-1)]
    select_n x1, other arithmetic: 0.11 us -> 1.18 us  [body(): cot = jnp.where(live, cotangent, jnp.zeros((), cotangent.dtype))]
where the time goes in v2:
time: 46.2 us; the launch traced here: 45.9 us
  Pallas kernels  37.7 us (82%)
  local copies, waits for them, and re-layouts  5.61 us (12%)
  other arithmetic  1.83 us (4%)
  between operations  0.75 us (2%)
    pallas_call x1, Pallas kernels, whole(): pl.pallas_call(functools.partial(whole_kernel, scale), out_shape=(jax.Sha...  37.7 us
    unnamed x9, local copies, waits for them, and re-layouts  3.01 us
    select_n x1, other arithmetic, body(): cot = jnp.where(live, cotangent, jnp.zeros((), cotangent.dtype))  1.18 us

profile of v2, /device:TPU:0, one launch (start us, length us, event | category | flops | bytes accessed | tf_op | source)
XLA Modules:
  0.0 45.9 jit_solution(17448454209160127729)
XLA Ops:
  0.6 0.0 copy-start.3
  0.6 0.6 %copy-done.3 = s32[32]{0:T(128)S(1)} copy-done((s32[32]{0:T(128)S(1)}, s32[32]{0:T(128)}, u32[]{:S(2)}) %copy-start.3) | copy-done | bytes 152
  1.3 0.6 %dynamic_slice.8 = s32[1]{0:T(128)} dynamic-slice(s32[32]{0:T(128)S(1)} %copy-done.3, s32[]{:T(128)S(6)} %select_n.10), dynamic_slice_sizes={1} | dynamic-slice | bytes 12 | tf_op jit(solution)/shard_map/dynamic_slice | solution.py:298
  1.9 0.6 %iota_compare_fusion = pred[4]{0:T(512)(128)(4,1)S(1)} fusion(s32[]{:T(128)} %bitcast.2), kind=kLoop, calls=%fused_computation.4 | loop fusion | flops 4 | bytes 8 | tf_op jit(solution)/shard_map/lt | solution.py:299
  2.5 1.2 %broadcast_select_fusion = bf16[4,9,8,8,128]{4,3,2,1,0:T(8,128)(2,1)S(1)} fusion(bf16[4,9,8,8,128]{4,3,2,1,0:T(8,128)(2,1)} %param.6, pred[4]{0:T(512)(128)(4,1)S(1)} %iota_compare_fusion), kind=kLoop, calls=%fused_computation | loop fusion | flops 294912 | bytes 1179652 | tf_op jit(solution)/shard_map/jit(_where)/select_n | solution.py:300
  3.7 0.4 copy.12
  4.1 0.0 copy-start.1
  4.1 0.1 copy.13.cot_ref
  4.2 0.8 %copy-done.1 = bf16[4,9,4,4,128]{4,3,2,1,0:T(4,128)(2,1)S(1)} copy-done((bf16[4,9,4,4,128]{4,3,2,1,0:T(4,128)(2,1)S(1)}, bf16[4,9,4,4,128]{4,3,2,1,0:T(4,128)(2,1)}, u32[]{:S(2)}) %copy-start.1) | copy-done | bytes 147480
  5.0 0.1 copy.11
  5.1 0.0 copy-start.2
  5.1 0.1 reshape.32.x_ref
  5.2 0.8 %copy-done.2 = bf16[432,128]{1,0:T(8,128)(2,1)S(1)} copy-done((bf16[432,128]{1,0:T(8,128)(2,1)S(1)}, bf16[432,128]{1,0:T(8,128)(2,1)}, u32[]{:S(2)}) %copy-start.2) | copy-done | bytes 110616
  6.1 0.0 copy-start
  6.1 0.6 %copy-done = f32[128]{0:T(128)S(1)} copy-done((f32[128]{0:T(128)S(1)}, f32[128]{0:T(128)}, u32[]{:S(2)}) %copy-start) | copy-done | bytes 536
  6.8 37.7 %shard_map.68 = (f32[4,7,16,128]{3,2,1,0:T(8,128)S(1)}, f32[8,128]{1,0:T(8,128)S(1)}) custom-call(bf16[27,16,128]{2,1,0:T(8,128)(2,1)S(1)} %bitcast.16, bf16[576,128]{1,0:T(8,128)(2,1)S(1)} %reshape.32.x_ref, bf16[4,576,128]{2,1,0:T(8,128)(2,1)S(1)} %copy.13.cot_ref, f32[1,128]{1,0:T(1,128)S(1)} %bitcast.18), custom_call_target="tpu_custom_call" | custom-call | tf_op jit(solution)/shard_map/pallas_call | solution.py:253
  44.5 0.6 %dynamic-slice_bitcast_fusion = f32[16]{0:T(128)} fusion(f32[1,128]{1,0:T(1,128)S(1)} %slice.7, s32[]{:T(128)S(6)} %select_n.12), kind=kLoop, calls=%fused_computation.3 | loop fusion | bytes 132 | tf_op jit(solution)/shard_map/dynamic_slice | solution.py:310
  45.1 0.1 copy.18
  45.2 0.7 %reshape.37 = f32[432,128]{1,0:T(8,128)} reshape(f32[16,27,128]{2,1,0:T(8,128)S(1)} %bitcast.21) | data formatting | bytes 442368 | tf_op jit(solution)/shard_map/reshape | solution.py:309
  (4 shorter events, 0.1 us)
Async XLA Ops:
  0.6 0.7 %copy-start.3 = (s32[32]{0:T(128)S(1)}, s32[32]{0:T(128)}, u32[]{:S(2)}) copy-start(s32[32]{0:T(128)} %param.9) | copy-start | bytes 388
  4.1 0.9 %copy-start.1 = (bf16[4,9,4,4,128]{4,3,2,1,0:T(4,128)(2,1)S(1)}, bf16[4,9,4,4,128]{4,3,2,1,0:T(4,128)(2,1)}, u32[]{:S(2)}) copy-start(bf16[4,9,4,4,128]{4,3,2,1,0:T(4,128)(2,1)} %param.5) | copy-start | bytes 442372
  5.1 0.9 %copy-start.2 = (bf16[432,128]{1,0:T(8,128)(2,1)S(1)}, bf16[432,128]{1,0:T(8,128)(2,1)}, u32[]{:S(2)}) copy-start(bf16[432,128]{1,0:T(8,128)(2,1)} %param.7) | copy-start | bytes 331780
  6.1 0.7 %copy-start = (f32[128]{0:T(128)S(1)}, f32[128]{0:T(128)}, u32[]{:S(2)}) copy-start(f32[128]{0:T(128)} %param.8) | copy-start | bytes 1540

commit v3 on v2

--- a/solution.py
+++ b/solution.py
@@ -66,9 +66,12 @@
                         )
 
 
-def products(xs_ref, cot_ref, bias_ref, wz_ref, g_ref):
+def products(count, xs_ref, cot_ref, bias_ref, wz_ref, g_ref):
     slab = xs_ref.shape[0] // 6
     rows = 4 * slab
+    row = lax.broadcasted_iota(jnp.int32, (rows, 128), 0).astype(jnp.float32)
+    place = row - 36.0 * jnp.floor((row + 0.5) * (1.0 / 36.0))
+    live = place < 9.0 * count.astype(jnp.float32)
     cols = ((0, 256), (0, 512), (256, 256))
 
     def window(dh):
@@ -84,7 +87,7 @@
         z = mid[:, p * 128 : p * 128 + 128] + side + bias_ref[...]
         sig = jax.nn.sigmoid(z)
         dz = cot_ref[p].astype(jnp.float32) * sig * (1.0 + z * (1.0 - sig))
-        dz = dz.astype(jnp.bfloat16)
+        dz = jnp.where(live, dz, 0.0).astype(jnp.bfloat16)
         total_b += jnp.sum(dz.astype(jnp.float32), axis=0, keepdims=True)
         parts.append(dz)
     dz = jnp.concatenate(parts, axis=1)
@@ -99,14 +102,16 @@
     return total_b
 
 
-def tap_gradient(g_ref, k):
+def tap_gradient(g_ref, k, base=0, size=128):
     kd, kh, kw = k // 9, k // 3 % 3, k % 3
     total = None
     for ph in range(2):
         for pw in range(2):
             row = (OFFSET[pw][kw] + pw) * 384 + kd * 128
             col = (2 * ph + pw) * 128
-            term = g_ref[OFFSET[ph][kh] + ph, row : row + 128, col : col + 128]
+            term = g_ref[
+                OFFSET[ph][kh] + ph, pl.ds(base + row, size), col : col + 128
+            ]
             total = term if total is None else total + term
     return total
 
@@ -119,29 +124,32 @@
 ]
 
 
-def terms_kernel(w_ref, x_ref, cot_ref, bias_ref, out_ref, f_ref, xs_ref, wz_ref, g_ref):
+def terms_kernel(
+    count_ref, w_ref, x_ref, cot_ref, bias_ref, out_ref, f_ref, xs_ref, wz_ref, g_ref
+):
     build_windows(x_ref, f_ref, xs_ref)
     wz_ref[...] = jnp.zeros_like(wz_ref)
     combine_weights(w_ref, wz_ref)
-    total_b = products(xs_ref, cot_ref, bias_ref, wz_ref, g_ref)
+    total_b = products(count_ref[0], xs_ref, cot_ref, bias_ref, wz_ref, g_ref)
     for k in range(27):
         out_ref[:, k] = tap_gradient(g_ref, k).reshape(8, 16, 128)
     out_ref[:, 27] = jnp.broadcast_to(total_b.reshape(1, 1, 128), (8, 16, 128))
 
 
-def terms(w, x, cot, bias):
+def terms(count, w, x, cot, bias):
     return pl.pallas_call(
         terms_kernel,
         out_shape=jax.ShapeDtypeStruct((8, 28, 16, 128), jnp.float32),
-        in_specs=[pl.BlockSpec(memory_space=pltpu.VMEM)] * 4,
+        in_specs=[pl.BlockSpec(memory_space=pltpu.SMEM)]
+        + [pl.BlockSpec(memory_space=pltpu.VMEM)] * 4,
         out_specs=pl.BlockSpec(memory_space=pltpu.VMEM),
         scratch_shapes=WORK,
         compiler_params=pltpu.CompilerParams(vmem_limit_bytes=48 * 2**20),
-    )(w, x, cot, bias)
+    )(count, w, x, cot, bias)
 
 
 def whole_kernel(
-    scale, w_ref, x_ref, cot_ref, bias_ref, o_ref, b_ref,
+    scale, counts_ref, w_ref, x_ref, cot_ref, bias_ref, o_ref, b_ref,
     f_ref, xs_ref, wz_ref, g_ref, w_all, parts,
     s1, r1, s2, r2, keep, s3, r3, s4, r4, sb, rb,
     sw1, rw1, sw2, rw2, ss1, rs1, ss2, rs2, ss3, rs3, ss4, rs4, ssb, rsb,
@@ -182,37 +190,62 @@
     for copy in swap:
         copy.wait_recv()
     combine_weights(w_all, wz_ref)
-    total_b = products(xs_ref, cot_ref, bias_ref, wz_ref, g_ref)
+    total_b = products(counts_ref[grp * 8 + dev], xs_ref, cot_ref, bias_ref, wz_ref, g_ref)
 
     sb[0] = jnp.broadcast_to(total_b, (8, 128))
     bias_copies = [send(sb.at[0], rb.at[0], ssb.at[0], rsb.at[0], pair)]
-    first = []
-    for q in range(4):
-        for k in range(7 * q, 7 * q + 7):
-            if k < 27:
-                parts[:, :, k] = tap_gradient(g_ref, k).reshape(4, 2, 16, 128)
+    first, second, third = [], [], []
+
+    def start_first(k):
+        base = pl.multiple_of(((depth + k + 1) % 4) * 32, 32)
+        for tap in range(27):
+            parts[k, :, tap] = tap_gradient(g_ref, tap, base, 32).reshape(2, 16, 128)
+        parts[k, :, 27] = jnp.zeros((2, 16, 128), f32)
+        s1[k] = parts[k, 1 - core].astype(bf16)
+        first.append(send(s1.at[k], r1.at[k], ss1.at[k], rs1.at[k], pair))
+
+    def start_second(k):
+        first[k].wait_recv()
+        for j in range(4):
+            taps = pl.ds(((grp + j + 1) % 4) * 7, 7)
+            total = parts[k, core, taps] + r1[k, taps].astype(f32)
+            if j < 3:
+                s2[k, j] = total.astype(bf16)
+                second.append(
+                    send(
+                        s2.at[k, j], r2.at[k, j], ss2.at[k, j], rs2.at[k, j], across[j]
+                    )
+                )
             else:
-                parts[:, :, k] = jnp.zeros((4, 2, 16, 128), f32)
-        s1[q] = parts[:, 1 - core, 7 * q : 7 * q + 7].astype(bf16)
-        first.append(send(s1.at[q], r1.at[q], ss1.at[q], rs1.at[q], pair))
-
+                keep[k] = total
+
+    def start_third(k):
+        total = keep[k]
+        for j in range(3):
+            second[3 * k + j].wait_recv()
+            total += r2[k, j].astype(f32)
+        if k < 3:
+            s3[k] = total.astype(bf16)
+            third.append(send(s3.at[k], r3.at[k], ss3.at[k], rs3.at[k], along[k]))
+        else:
+            keep[k] = total
+
+    start_first(0)
+    start_first(1)
+    start_second(0)
+    start_first(2)
     bias_copies[0].wait_recv()
     sb[1] = sb[0] + rb[0]
     for k in range(3):
         bias_copies.append(
             send(sb.at[1], rb.at[1 + k], ssb.at[1 + k], rsb.at[1 + k], across[k])
         )
-    second = []
-    for q in range(4):
-        first[q].wait_recv()
-    for k in range(4):
-        q = (grp + k + 1) % 4
-        total = parts[:, core, pl.ds(q * 7, 7)] + r1[q].astype(f32)
-        if k < 3:
-            s2[k] = total.astype(bf16)
-            second.append(send(s2.at[k], r2.at[k], ss2.at[k], rs2.at[k], across[k]))
-        else:
-            keep[...] = total
+    start_second(1)
+    start_first(3)
+    start_second(2)
+    start_third(0)
+    start_second(3)
+    start_third(1)
     for k in range(3):
         bias_copies[1 + k].wait_recv()
     sb[2] = (sb[1] + rb[1]) + (rb[2] + rb[3])
@@ -220,17 +253,12 @@
         bias_copies.append(
             send(sb.at[2], rb.at[4 + k], ssb.at[4 + k], rsb.at[4 + k], along[k])
         )
-    for k in range(3):
-        second[k].wait_recv()
-        keep[...] += r2[k].astype(f32)
-    third = []
-    for k in range(3):
-        s3[k] = keep[(depth + k + 1) % 4].astype(bf16)
-        third.append(send(s3.at[k], r3.at[k], ss3.at[k], rs3.at[k], along[k]))
+    start_third(2)
+    start_third(3)
     for k in range(3):
         bias_copies[4 + k].wait_recv()
     b_ref[...] = ((sb[2] + rb[4]) + (rb[5] + rb[6])) * scale
-    total = keep[depth]
+    total = keep[3]
     for k in range(3):
         third[k].wait_recv()
         total += r3[k].astype(f32)
@@ -247,7 +275,7 @@
         copy.wait_send()
 
 
-def whole(w, x, cot, bias, scale):
+def whole(counts, w, x, cot, bias, scale):
     bf16, f32 = jnp.bfloat16, jnp.float32
     sem = pltpu.SemaphoreType.DMA
     return pl.pallas_call(
@@ -256,16 +284,17 @@
             jax.ShapeDtypeStruct((4, 7, 16, 128), f32),
             jax.ShapeDtypeStruct((8, 128), f32),
         ),
-        in_specs=[pl.BlockSpec(memory_space=pltpu.VMEM)] * 4,
+        in_specs=[pl.BlockSpec(memory_space=pltpu.SMEM)]
+        + [pl.BlockSpec(memory_space=pltpu.VMEM)] * 4,
         out_specs=[pl.BlockSpec(memory_space=pltpu.VMEM)] * 2,
         scratch_shapes=WORK
         + [
             pltpu.VMEM((8, 27, 16, 128), bf16),
             pltpu.VMEM((4, 2, 28, 16, 128), f32),
-            pltpu.VMEM((4, 4, 7, 16, 128), bf16),
-            pltpu.VMEM((4, 4, 7, 16, 128), bf16),
-            pltpu.VMEM((3, 4, 7, 16, 128), bf16),
-            pltpu.VMEM((3, 4, 7, 16, 128), bf16),
+            pltpu.VMEM((4, 28, 16, 128), bf16),
+            pltpu.VMEM((4, 28, 16, 128), bf16),
+            pltpu.VMEM((4, 3, 7, 16, 128), bf16),
+            pltpu.VMEM((4, 3, 7, 16, 128), bf16),
             pltpu.VMEM((4, 7, 16, 128), f32),
             pltpu.VMEM((3, 7, 16, 128), bf16),
             pltpu.VMEM((3, 7, 16, 128), bf16),
@@ -274,14 +303,14 @@
             pltpu.VMEM((3, 8, 128), f32),
             pltpu.VMEM((7, 8, 128), f32),
             sem((3,)), sem((3,)), sem((4,)), sem((4,)),
-            sem((4,)), sem((4,)), sem((3,)), sem((3,)),
+            sem((4,)), sem((4,)), sem((4, 3)), sem((4, 3)),
             sem((3,)), sem((3,)), sem((3,)), sem((3,)),
             sem((7,)), sem((7,)),
         ],
         compiler_params=pltpu.CompilerParams(
             collective_id=1, has_side_effects=True, vmem_limit_bytes=48 * 2**20
         ),
-    )(w, x, cot, bias)
+    )(counts, w, x, cot, bias)
 
 
 def body(tiles, cotangent, weight, bias, counts):
@@ -295,16 +324,13 @@
 
     mine = weight.reshape(cin // num_dev, 27, cout).transpose(1, 0, 2)
     x = tiles.transpose(2, 3, 0, 1, 4).reshape(hl * wl * cap * frames, cin)
-    my_count = counts[my_grp * num_dev + my_dev]
-    live = (jnp.arange(cap, dtype=jnp.int32) < my_count).reshape(cap, 1, 1, 1, 1)
-    cot = jnp.where(live, cotangent, jnp.zeros((), cotangent.dtype))
-    cot = cot.reshape(cap, frames, hl, 2, wl, 2, cout).transpose(3, 5, 2, 4, 0, 1, 6)
+    cot = cotangent.reshape(cap, frames, hl, 2, wl, 2, cout).transpose(3, 5, 2, 4, 0, 1, 6)
     cot = cot.reshape(4, hl * wl * cap * frames, cout)
 
     share = cout // num_dev
     bias = bias.reshape(1, cout)
     if (num_grp, num_dev) == (4, 8):
-        done, total_b = whole(mine, x, cot, bias, scale)
+        done, total_b = whole(counts, mine, x, cot, bias, scale)
         done = done.reshape(28, 16, cout)
         part_w = done[:27].transpose(1, 0, 2).reshape(432, cout)
         part_b = lax.dynamic_slice_in_dim(total_b[0], my_dev * share, share, 0)
@@ -313,7 +339,8 @@
     if num_dev != 8:
         gathered = gathered.transpose(1, 0, 2, 3).reshape(27, 8, 16, cout)
         gathered = gathered.transpose(1, 0, 2, 3)
-    parts = terms(gathered, x, cot, bias)
+    count = lax.dynamic_slice_in_dim(counts, my_grp * num_dev + my_dev, 1)
+    parts = terms(count, gathered, x, cot, bias)
     flat = parts[:, :27].transpose(0, 2, 1, 3).reshape(cin * 27, cout)
     part_w = lax.psum_scatter(flat, "dev", scatter_dimension=0, tiled=True)
     part_w = lax.psum(part_w, "grp")

time: 46.2 us -> 43.2 us (0.935)
  other arithmetic: 1.83 us -> 0 us
  Pallas kernels: 37.7 us -> 36.8 us
    select_n x1 -> x0, other arithmetic: 1.18 us -> none  [body(): cot = jnp.where(live, cotangent, jnp.zeros((), cotangent.dtype))]
    reshape x1, local copies, waits for them, and re-layouts: 0.41 us -> 1.47 us  [body(): cotangent.reshape(cap, frames, hl, 2, wl, 2, cout)]
    pallas_call x1, Pallas kernels: 37.7 us -> 36.8 us  [whole(): pl.pallas_call(functools.partial(whole_kernel, scale), out_shape=(jax.Sha...]
    lt x1 -> x0, other arithmetic: 0.65 us -> none  [body(): jnp.arange(cap, dtype=jnp.int32) < my_count]
    unnamed x9, local copies, waits for them, and re-layouts: 3.01 us -> 2.36 us
    dynamic_slice x1 -> x0, local copies, waits for them, and re-layouts: 0.58 us -> none  [body(): my_count = counts[my_grp * num_dev + my_dev]]
where the time goes in v3:
time: 43.2 us; the launch traced here: 42.9 us
  Pallas kernels  36.8 us (85%)
  local copies, waits for them, and re-layouts  5.45 us (13%)
  between operations  0.73 us (2%)
    pallas_call x1, Pallas kernels, whole(): pl.pallas_call(functools.partial(whole_kernel, scale), out_shape=(jax.Sha...  36.8 us
    unnamed x9, local copies, waits for them, and re-layouts  2.36 us
    reshape x1, local copies, waits for them, and re-layouts, body(): cotangent.reshape(cap, frames, hl, 2, wl, 2, cout)  1.47 us

profile of v3, /device:TPU:0, one launch (start us, length us, event | category | flops | bytes accessed | tf_op | source)
XLA Modules:
  0.0 42.9 jit_solution(13644033941241588017)
XLA Ops:
  0.6 1.5 %copy.12 = bf16[4,9,4,2,4,2,128]{6,5,3,1,0,4,2:T(2,128)(2,1)S(1)} copy(bf16[4,9,4,2,4,2,128]{6,5,4,3,2,1,0:T(2,128)(2,1)} %bitcast.20) | data formatting | bytes 1179648 | tf_op jit(solution)/shard_map/reshape | solution.py:327
  2.1 0.0 copy-start.2
  2.1 0.1 copy.13.cot_ref
  2.2 0.8 %copy-done.2 = bf16[4,9,4,4,128]{4,3,2,1,0:T(4,128)(2,1)S(1)} copy-done((bf16[4,9,4,4,128]{4,3,2,1,0:T(4,128)(2,1)S(1)}, bf16[4,9,4,4,128]{4,3,2,1,0:T(4,128)(2,1)}, u32[]{:S(2)}) %copy-start.2) | copy-done | bytes 147480
  3.0 0.1 copy.11
  3.1 0.0 copy-start.3
  3.1 0.1 reshape.27.x_ref
  3.2 0.8 %copy-done.3 = bf16[432,128]{1,0:T(8,128)(2,1)S(1)} copy-done((bf16[432,128]{1,0:T(8,128)(2,1)S(1)}, bf16[432,128]{1,0:T(8,128)(2,1)}, u32[]{:S(2)}) %copy-start.3) | copy-done | bytes 110616
  4.1 0.0 copy-start
  4.1 0.0 copy-start.1
  4.1 0.6 %copy-done = s32[32]{0:T(128)S(1)} copy-done((s32[32]{0:T(128)S(1)}, s32[32]{0:T(128)}, u32[]{:S(2)}) %copy-start) | copy-done | bytes 152
  4.8 0.0 copy-done.1
  4.8 36.8 %shard_map.68 = (f32[4,7,16,128]{3,2,1,0:T(8,128)S(1)}, f32[8,128]{1,0:T(8,128)S(1)}) custom-call(s32[32]{0:T(128)S(1)} %copy-done, bf16[27,16,128]{2,1,0:T(8,128)(2,1)S(1)} %bitcast.15, bf16[576,128]{1,0:T(8,128)(2,1)S(1)} %reshape.27.x_ref, bf16[4,576,128]{2,1,0:T(8,128)(2,1)S(1)} %copy.13.cot_ref, f32[1,128]{1,0:T(1,128)S(1)} %bitcast.17), custom_call_target="tpu_custom_call" | custom-call | tf_op jit(solution)/shard_map/pallas_call | solution.py:281
  41.5 0.6 %dynamic-slice_bitcast_fusion = f32[16]{0:T(128)} fusion(f32[1,128]{1,0:T(1,128)S(1)} %slice.7, s32[]{:T(128)S(6)} %select_n.3), kind=kLoop, calls=%fused_computation.2 | loop fusion | bytes 132 | tf_op jit(solution)/shard_map/dynamic_slice | solution.py:336
  42.1 0.1 copy.18
  42.2 0.7 %reshape.32 = f32[432,128]{1,0:T(8,128)} reshape(f32[16,27,128]{2,1,0:T(8,128)S(1)} %bitcast.19) | data formatting | bytes 442368 | tf_op jit(solution)/shard_map/reshape | solution.py:335
  (4 shorter events, 0.1 us)
Async XLA Ops:
  2.1 0.9 %copy-start.2 = (bf16[4,9,4,4,128]{4,3,2,1,0:T(4,128)(2,1)S(1)}, bf16[4,9,4,4,128]{4,3,2,1,0:T(4,128)(2,1)}, u32[]{:S(2)}) copy-start(bf16[4,9,4,4,128]{4,3,2,1,0:T(4,128)(2,1)} %param.5) | copy-start | bytes 442372
  3.1 0.9 %copy-start.3 = (bf16[432,128]{1,0:T(8,128)(2,1)S(1)}, bf16[432,128]{1,0:T(8,128)(2,1)}, u32[]{:S(2)}) copy-start(bf16[432,128]{1,0:T(8,128)(2,1)} %param.7) | copy-start | bytes 331780
  4.1 0.7 %copy-start = (s32[32]{0:T(128)S(1)}, s32[32]{0:T(128)}, u32[]{:S(2)}) copy-start(s32[32]{0:T(128)} %counts_ref.1) | copy-start | bytes 388
  4.1 0.7 %copy-start.1 = (f32[128]{0:T(128)S(1)}, f32[128]{0:T(128)}, u32[]{:S(2)}) copy-start(f32[128]{0:T(128)} %param.8) | copy-start | bytes 1540

commit v4 on v3

--- a/solution.py
+++ b/solution.py
@@ -149,10 +149,10 @@
 
 
 def whole_kernel(
-    scale, counts_ref, w_ref, x_ref, cot_ref, bias_ref, o_ref, b_ref,
+    scale, counts_ref, w_ref, x_ref, cot_any, bias_ref, o_ref, b_ref,
     f_ref, xs_ref, wz_ref, g_ref, w_all, parts,
     s1, r1, s2, r2, keep, s3, r3, s4, r4, sb, rb,
-    sw1, rw1, sw2, rw2, ss1, rs1, ss2, rs2, ss3, rs3, ss4, rs4, ssb, rsb,
+    cot_ref, fetch_sem, sw3, rw3, sw1, rw1, sw2, rw2, ss1, rs1, ss2, rs2, ss3, rs3, ss4, rs4, ssb, rsb,
 ):
     grp = lax.axis_index("grp")
     dev = lax.axis_index("dev")
@@ -176,20 +176,36 @@
         copy.start()
         return copy
 
+    fetch = pltpu.make_async_copy(cot_any, cot_ref, fetch_sem)
+    fetch.start()
+    quarter = pl.ds(grp * 7, 7)
     out = [
-        send(w_ref, w_all.at[dev], sw1.at[k], rw1.at[k], along[k]) for k in range(3)
+        send(
+            w_ref.at[quarter], w_all.at[dev, quarter], sw1.at[k], rw1.at[k], along[k]
+        )
+        for k in (0, 2, 1)
     ]
     swap = [send(w_ref, w_all.at[dev], sw2.at[3], rw2.at[3], pair)]
     w_all[dev] = w_ref[...]
     wz_ref[...] = jnp.zeros_like(wz_ref)
+    spread = []
+    for i, k in enumerate((0, 2, 1)):
+        out[i].wait_recv()
+        block = w_all.at[((depth + 3 - k) % 4) * 2 + core, quarter]
+        for j in range(3):
+            spread.append(
+                send(block, block, sw3.at[k, j], rw3.at[k, j], across[j])
+            )
     build_windows(x_ref, f_ref, xs_ref)
-    for k in (0, 2, 1):
-        out[k].wait_recv()
+    for i, k in enumerate((0, 2, 1)):
+        for j in range(3):
+            spread[3 * i + j].wait_recv()
         block = w_all.at[((depth + 3 - k) % 4) * 2 + core]
         swap.append(send(block, block, sw2.at[k], rw2.at[k], pair))
     for copy in swap:
         copy.wait_recv()
     combine_weights(w_all, wz_ref)
+    fetch.wait()
     total_b = products(counts_ref[grp * 8 + dev], xs_ref, cot_ref, bias_ref, wz_ref, g_ref)
 
     sb[0] = jnp.broadcast_to(total_b, (8, 128))
@@ -271,7 +287,7 @@
     for k in range(3):
         fourth[k].wait_recv()
         o_ref[(grp + 3 - k) % 4] = r4[k]
-    for copy in out + swap + bias_copies + first + second + third + fourth:
+    for copy in out + spread + swap + bias_copies + first + second + third + fourth:
         copy.wait_send()
 
 
@@ -285,11 +301,13 @@
             jax.ShapeDtypeStruct((8, 128), f32),
         ),
         in_specs=[pl.BlockSpec(memory_space=pltpu.SMEM)]
-        + [pl.BlockSpec(memory_space=pltpu.VMEM)] * 4,
+        + [pl.BlockSpec(memory_space=pltpu.VMEM)] * 2
+        + [pl.BlockSpec(memory_space=pl.ANY)]
+        + [pl.BlockSpec(memory_space=pltpu.VMEM)],
         out_specs=[pl.BlockSpec(memory_space=pltpu.VMEM)] * 2,
         scratch_shapes=WORK
         + [
-            pltpu.VMEM((8, 27, 16, 128), bf16),
+            pltpu.VMEM((8, 28, 16, 128), bf16),
             pltpu.VMEM((4, 2, 28, 16, 128), f32),
             pltpu.VMEM((4, 28, 16, 128), bf16),
             pltpu.VMEM((4, 28, 16, 128), bf16),
@@ -302,6 +320,8 @@
             pltpu.VMEM((3, 7, 16, 128), f32),
             pltpu.VMEM((3, 8, 128), f32),
             pltpu.VMEM((7, 8, 128), f32),
+            pltpu.VMEM((4, 576, 128), bf16),
+            sem, sem((3, 3)), sem((3, 3)),
             sem((3,)), sem((3,)), sem((4,)), sem((4,)),
             sem((4,)), sem((4,)), sem((4, 3)), sem((4, 3)),
             sem((3,)), sem((3,)), sem((3,)), sem((3,)),
@@ -330,6 +350,7 @@
     share = cout // num_dev
     bias = bias.reshape(1, cout)
     if (num_grp, num_dev) == (4, 8):
+        mine = jnp.pad(mine, ((0, 1), (0, 0), (0, 0)))
         done, total_b = whole(counts, mine, x, cot, bias, scale)
         done = done.reshape(28, 16, cout)
         part_w = done[:27].transpose(1, 0, 2).reshape(432, cout)

time: 43.2 us -> 41.1 us (0.951)
  Pallas kernels: 36.8 us -> 34.6 us
    pallas_call x1, Pallas kernels: 36.8 us -> 34.6 us  [whole(): pl.pallas_call(functools.partial(whole_kernel, scale), out_shape=(jax.Sha...]
where the time goes in v4:
time: 41.1 us; the launch traced here: 40.9 us
  Pallas kernels  34.6 us (84%)
  local copies, waits for them, and re-layouts  5.46 us (13%)
  between operations  0.74 us (2%)
    pallas_call x1, Pallas kernels, whole(): pl.pallas_call(functools.partial(whole_kernel, scale), out_shape=(jax.Sha...  34.6 us
    unnamed x9, local copies, waits for them, and re-layouts  2.36 us
    reshape x1, local copies, waits for them, and re-layouts, body(): cotangent.reshape(cap, frames, hl, 2, wl, 2, cout)  1.47 us

profile of v4, /device:TPU:0, one launch (start us, length us, event | category | flops | bytes accessed | tf_op | source)
XLA Modules:
  0.0 40.9 jit_solution(5006984392357941428)
XLA Ops:
  0.6 1.5 %copy.12 = bf16[4,9,4,2,4,2,128]{6,5,3,1,0,4,2:T(2,128)(2,1)S(1)} copy(bf16[4,9,4,2,4,2,128]{6,5,4,3,2,1,0:T(2,128)(2,1)} %bitcast.19) | data formatting | bytes 1179648 | tf_op jit(solution)/shard_map/reshape | solution.py:347
  2.1 0.0 copy-start.2
  2.1 0.1 copy.13.cot_any
  2.2 0.8 %copy-done.2 = bf16[4,9,4,4,128]{4,3,2,1,0:T(4,128)(2,1)S(1)} copy-done((bf16[4,9,4,4,128]{4,3,2,1,0:T(4,128)(2,1)S(1)}, bf16[4,9,4,4,128]{4,3,2,1,0:T(4,128)(2,1)}, u32[]{:S(2)}) %copy-start.2) | copy-done | bytes 147480
  3.0 0.1 copy.11
  3.1 0.0 copy-start.3
  3.1 0.1 reshape.27.x_ref
  3.2 0.8 %copy-done.3 = bf16[432,128]{1,0:T(8,128)(2,1)S(1)} copy-done((bf16[432,128]{1,0:T(8,128)(2,1)S(1)}, bf16[432,128]{1,0:T(8,128)(2,1)}, u32[]{:S(2)}) %copy-start.3) | copy-done | bytes 110616
  4.1 0.0 copy-start
  4.1 0.0 copy-start.1
  4.1 0.6 %copy-done = s32[32]{0:T(128)S(1)} copy-done((s32[32]{0:T(128)S(1)}, s32[32]{0:T(128)}, u32[]{:S(2)}) %copy-start) | copy-done | bytes 152
  4.8 0.0 copy-done.1
  4.8 34.6 %shard_map.68 = (f32[4,7,16,128]{3,2,1,0:T(8,128)S(1)}, f32[8,128]{1,0:T(8,128)S(1)}) custom-call(s32[32]{0:T(128)S(1)} %copy-done, bf16[28,16,128]{2,1,0:T(8,128)(2,1)S(1)} %pad.4.w_ref, bf16[576,128]{1,0:T(8,128)(2,1)S(1)} %reshape.27.x_ref, bf16[4,576,128]{2,1,0:T(8,128)(2,1)S(1)} %copy.13.cot_any, f32[1,128]{1,0:T(1,128)S(1)} %bitcast.16), custom_call_target="tpu_custom_call" | custom-call | tf_op jit(solution)/shard_map/pallas_call | solution.py:297
  39.5 0.6 %dynamic-slice_bitcast_fusion = f32[16]{0:T(128)} fusion(f32[1,128]{1,0:T(1,128)S(1)} %slice.7, s32[]{:T(128)S(6)} %select_n.3), kind=kLoop, calls=%fused_computation.2 | loop fusion | bytes 132 | tf_op jit(solution)/shard_map/dynamic_slice | solution.py:357
  40.1 0.1 copy.18
  40.1 0.7 %reshape.32 = f32[432,128]{1,0:T(8,128)} reshape(f32[16,27,128]{2,1,0:T(8,128)S(1)} %bitcast.18) | data formatting | bytes 442368 | tf_op jit(solution)/shard_map/reshape | solution.py:356
  (5 shorter events, 0.1 us)
Async XLA Ops:
  2.1 0.9 %copy-start.2 = (bf16[4,9,4,4,128]{4,3,2,1,0:T(4,128)(2,1)S(1)}, bf16[4,9,4,4,128]{4,3,2,1,0:T(4,128)(2,1)}, u32[]{:S(2)}) copy-start(bf16[4,9,4,4,128]{4,3,2,1,0:T(4,128)(2,1)} %param.5) | copy-start | bytes 442372
  3.1 0.9 %copy-start.3 = (bf16[432,128]{1,0:T(8,128)(2,1)S(1)}, bf16[432,128]{1,0:T(8,128)(2,1)}, u32[]{:S(2)}) copy-start(bf16[432,128]{1,0:T(8,128)(2,1)} %param.7) | copy-start | bytes 331780
  4.1 0.7 %copy-start = (s32[32]{0:T(128)S(1)}, s32[32]{0:T(128)}, u32[]{:S(2)}) copy-start(s32[32]{0:T(128)} %counts_ref.1) | copy-start | bytes 388
  4.1 0.7 %copy-start.1 = (f32[128]{0:T(128)S(1)}, f32[128]{0:T(128)}, u32[]{:S(2)}) copy-start(f32[128]{0:T(128)} %param.8) | copy-start | bytes 1540

commit v5 on v4

--- a/solution.py
+++ b/solution.py
@@ -149,10 +149,10 @@
 
 
 def whole_kernel(
-    scale, counts_ref, w_ref, x_ref, cot_any, bias_ref, o_ref, b_ref,
+    scale, counts_ref, w_ref, x_any, cot_any, bias_ref, o_ref, b_ref,
     f_ref, xs_ref, wz_ref, g_ref, w_all, parts,
     s1, r1, s2, r2, keep, s3, r3, s4, r4, sb, rb,
-    cot_ref, fetch_sem, sw3, rw3, sw1, rw1, sw2, rw2, ss1, rs1, ss2, rs2, ss3, rs3, ss4, rs4, ssb, rsb,
+    cot_ref, fetch_sem, x_ref, x_sem, sw3, rw3, sw1, rw1, sw2, rw2, ss1, rs1, ss2, rs2, ss3, rs3, ss4, rs4, ssb, rsb,
 ):
     grp = lax.axis_index("grp")
     dev = lax.axis_index("dev")
@@ -163,6 +163,10 @@
     across = [{"grp": (grp + k) % 4} for k in range(1, 4)]
     along = [{"dev": ((depth + k) % 4) * 2 + core} for k in range(1, 4)]
 
+    fetch_x = pltpu.make_async_copy(x_any, x_ref, x_sem)
+    fetch_x.start()
+    fetch = pltpu.make_async_copy(cot_any, cot_ref, fetch_sem)
+    fetch.start()
     barrier = pltpu.get_barrier_semaphore()
     for peer in [pair] + across + along:
         pl.semaphore_signal(barrier, inc=1, device_id=peer, device_id_type=MESH)
@@ -176,8 +180,6 @@
         copy.start()
         return copy
 
-    fetch = pltpu.make_async_copy(cot_any, cot_ref, fetch_sem)
-    fetch.start()
     quarter = pl.ds(grp * 7, 7)
     out = [
         send(
@@ -196,6 +198,7 @@
             spread.append(
                 send(block, block, sw3.at[k, j], rw3.at[k, j], across[j])
             )
+    fetch_x.wait()
     build_windows(x_ref, f_ref, xs_ref)
     for i, k in enumerate((0, 2, 1)):
         for j in range(3):
@@ -301,8 +304,8 @@
             jax.ShapeDtypeStruct((8, 128), f32),
         ),
         in_specs=[pl.BlockSpec(memory_space=pltpu.SMEM)]
-        + [pl.BlockSpec(memory_space=pltpu.VMEM)] * 2
-        + [pl.BlockSpec(memory_space=pl.ANY)]
+        + [pl.BlockSpec(memory_space=pltpu.VMEM)]
+        + [pl.BlockSpec(memory_space=pl.ANY)] * 2
         + [pl.BlockSpec(memory_space=pltpu.VMEM)],
         out_specs=[pl.BlockSpec(memory_space=pltpu.VMEM)] * 2,
         scratch_shapes=WORK
@@ -321,7 +324,7 @@
             pltpu.VMEM((3, 8, 128), f32),
             pltpu.VMEM((7, 8, 128), f32),
             pltpu.VMEM((4, 576, 128), bf16),
-            sem, sem((3, 3)), sem((3, 3)),
+            sem, pltpu.VMEM((576, 128), bf16), sem, sem((3, 3)), sem((3, 3)),
             sem((3,)), sem((3,)), sem((4,)), sem((4,)),
             sem((4,)), sem((4,)), sem((4, 3)), sem((4, 3)),
             sem((3,)), sem((3,)), sem((3,)), sem((3,)),

time: 41.1 us -> 41.3 us (level)
  no operation moved by 1% of the time
where the time goes in v5:
time: 41.3 us; the launch traced here: 41 us
  Pallas kernels  34.8 us (84%)
  local copies, waits for them, and re-layouts  5.46 us (13%)
  between operations  0.74 us (2%)
    pallas_call x1, Pallas kernels, whole(): pl.pallas_call(functools.partial(whole_kernel, scale), out_shape=(jax.Sha...  34.8 us
    unnamed x9, local copies, waits for them, and re-layouts  2.36 us
    reshape x1, local copies, waits for them, and re-layouts, body(): cotangent.reshape(cap, frames, hl, 2, wl, 2, cout)  1.47 us

profile of v5, /device:TPU:0, one launch (start us, length us, event | category | flops | bytes accessed | tf_op | source)
XLA Modules:
  0.0 41.0 jit_solution(10450246771778197436)
XLA Ops:
  0.6 1.5 %copy.12 = bf16[4,9,4,2,4,2,128]{6,5,3,1,0,4,2:T(2,128)(2,1)S(1)} copy(bf16[4,9,4,2,4,2,128]{6,5,4,3,2,1,0:T(2,128)(2,1)} %bitcast.19) | data formatting | bytes 1179648 | tf_op jit(solution)/shard_map/reshape | solution.py:350
  2.1 0.0 copy-start.2
  2.1 0.1 copy.13.cot_any
  2.2 0.8 %copy-done.2 = bf16[4,9,4,4,128]{4,3,2,1,0:T(4,128)(2,1)S(1)} copy-done((bf16[4,9,4,4,128]{4,3,2,1,0:T(4,128)(2,1)S(1)}, bf16[4,9,4,4,128]{4,3,2,1,0:T(4,128)(2,1)}, u32[]{:S(2)}) %copy-start.2) | copy-done | bytes 147480
  3.0 0.1 copy.11
  3.1 0.0 copy-start.3
  3.1 0.1 reshape.27.x_any
  3.2 0.8 %copy-done.3 = bf16[432,128]{1,0:T(8,128)(2,1)S(1)} copy-done((bf16[432,128]{1,0:T(8,128)(2,1)S(1)}, bf16[432,128]{1,0:T(8,128)(2,1)}, u32[]{:S(2)}) %copy-start.3) | copy-done | bytes 110616
  4.1 0.0 copy-start
  4.1 0.0 copy-start.1
  4.1 0.6 %copy-done = s32[32]{0:T(128)S(1)} copy-done((s32[32]{0:T(128)S(1)}, s32[32]{0:T(128)}, u32[]{:S(2)}) %copy-start) | copy-done | bytes 152
  4.8 0.0 copy-done.1
  4.8 34.8 %shard_map.68 = (f32[4,7,16,128]{3,2,1,0:T(8,128)S(1)}, f32[8,128]{1,0:T(8,128)S(1)}) custom-call(s32[32]{0:T(128)S(1)} %copy-done, bf16[28,16,128]{2,1,0:T(8,128)(2,1)S(1)} %pad.4.w_ref, bf16[576,128]{1,0:T(8,128)(2,1)S(1)} %reshape.27.x_any, bf16[4,576,128]{2,1,0:T(8,128)(2,1)S(1)} %copy.13.cot_any, f32[1,128]{1,0:T(1,128)S(1)} %bitcast.16), custom_call_target="tpu_custom_call" | custom-call | tf_op jit(solution)/shard_map/pallas_call | solution.py:300
  39.6 0.6 %dynamic-slice_bitcast_fusion = f32[16]{0:T(128)} fusion(f32[1,128]{1,0:T(1,128)S(1)} %slice.7, s32[]{:T(128)S(6)} %select_n.3), kind=kLoop, calls=%fused_computation.2 | loop fusion | bytes 132 | tf_op jit(solution)/shard_map/dynamic_slice | solution.py:360
  40.3 0.1 copy.18
  40.3 0.7 %reshape.32 = f32[432,128]{1,0:T(8,128)} reshape(f32[16,27,128]{2,1,0:T(8,128)S(1)} %bitcast.18) | data formatting | bytes 442368 | tf_op jit(solution)/shard_map/reshape | solution.py:359
  (5 shorter events, 0.1 us)
Async XLA Ops:
  2.1 0.9 %copy-start.2 = (bf16[4,9,4,4,128]{4,3,2,1,0:T(4,128)(2,1)S(1)}, bf16[4,9,4,4,128]{4,3,2,1,0:T(4,128)(2,1)}, u32[]{:S(2)}) copy-start(bf16[4,9,4,4,128]{4,3,2,1,0:T(4,128)(2,1)} %param.5) | copy-start | bytes 442372
  3.1 0.9 %copy-start.3 = (bf16[432,128]{1,0:T(8,128)(2,1)S(1)}, bf16[432,128]{1,0:T(8,128)(2,1)}, u32[]{:S(2)}) copy-start(bf16[432,128]{1,0:T(8,128)(2,1)} %param.7) | copy-start | bytes 331780
  4.1 0.7 %copy-start = (s32[32]{0:T(128)S(1)}, s32[32]{0:T(128)}, u32[]{:S(2)}) copy-start(s32[32]{0:T(128)} %counts_ref.1) | copy-start | bytes 388
  4.1 0.7 %copy-start.1 = (f32[128]{0:T(128)S(1)}, f32[128]{0:T(128)}, u32[]{:S(2)}) copy-start(f32[128]{0:T(128)} %param.8) | copy-start | bytes 1540
